TPU v7x, 32 devices: a whole 2x2x4 slice. The times are simulated.
32 devices in a mesh: seq: 8 (over z, x), chan: 4 (over y, core).
Axes of the slice: x: 2, y: 2, z: 4, core: 2. Of those that a mesh axis runs over, the one named last changes fastest.
Arguments:
- signal: float32 [256, 65536], P('chan', 'seq'), may hold values from -6 to 6
- gating: float32 [256, 65536], P('chan', 'seq'), may hold values from -6 to 6
- response: float32 [256, 65536], P('chan', 'seq'), may hold values from -0.0234375 to 0.0234375
- skip_gain: float32 [256], P('chan'), may hold values from -4 to 4
- mixing_weight: float32 [256, 256], P(None, 'chan'), may hold values from -0.5 to 0.5
Outputs:
- output: float32 [256, 65536], P('chan', 'seq')
All inputs are finite; a program needn't handle non-finite values.
Results may differ from a plain program's by a relative error of at most 0.00007.
Values sent between devices are 32-bit elements; how exact they have to be, the bound alone decides.
A program may use at most 128 MiB of HBM per device.

v0:
```python
from functools import partial
import math
import jax
import jax.numpy as jnp
import numpy as np
from jax import lax
from jax.sharding import PartitionSpec as P


def twiddle(number, period):
    angle = (number % period).astype(jnp.float32) * (2.0 * math.pi / period)
    return (jnp.cos(angle), jnp.sin(angle))


def rotate(real_part, imag_part, cos_part, sin_part):
    return (
        real_part * cos_part - imag_part * sin_part,
        imag_part * cos_part + real_part * sin_part,
    )


def dft_table(length, sign):
    steps = jnp.arange(length, dtype=jnp.int32)
    cos_part, sin_part = twiddle(steps[:, None] * steps[None, :], length)
    return (cos_part, sign * sin_part)


def complex_apply(pattern, table_real, table_imag, real_part, imag_part):
    contract = partial(jnp.einsum, pattern, precision=lax.Precision.HIGHEST)
    return (
        contract(table_real, real_part) - contract(table_imag, imag_part),
        contract(table_real, imag_part) + contract(table_imag, real_part),
    )


def spectral_order(length):
    if length <= 256:
        return np.arange(length)
    outer_len = length // 128
    return (spectral_order(outer_len)[:, None] + outer_len * np.arange(128)[None, :]).reshape(-1)


def whole_forward(real_part, imag_part, length):
    if length <= 256:
        table_real, table_imag = dft_table(length, -1.0)
        return complex_apply("kn,...n->...k", table_real, table_imag, real_part, imag_part)
    inner_len = 128
    outer_len = length // inner_len
    lead = real_part.shape[:-1]
    real_part = jnp.swapaxes(real_part.reshape(lead + (outer_len, inner_len)), -1, -2)
    imag_part = jnp.swapaxes(imag_part.reshape(lead + (outer_len, inner_len)), -1, -2)
    real_part, imag_part = whole_forward(real_part, imag_part, outer_len)
    real_part = jnp.swapaxes(real_part, -1, -2)
    imag_part = jnp.swapaxes(imag_part, -1, -2)
    freq_idx = jnp.asarray(spectral_order(outer_len), dtype=jnp.int32)[:, None]
    inner_idx = jnp.arange(inner_len, dtype=jnp.int32)[None, :]
    cos_part, sin_part = twiddle(freq_idx * inner_idx, length)
    real_part, imag_part = rotate(real_part, imag_part, cos_part, -sin_part)
    table_real, table_imag = dft_table(inner_len, -1.0)
    real_part, imag_part = complex_apply(
        "ub,...tb->...tu", table_real, table_imag, real_part, imag_part
    )
    return (real_part.reshape(lead + (length,)), imag_part.reshape(lead + (length,)))


def whole_inverse(real_part, imag_part, length):
    if length <= 256:
        table_real, table_imag = dft_table(length, 1.0)
        return complex_apply("kn,...n->...k", table_real, table_imag, real_part, imag_part)
    inner_len = 128
    outer_len = length // inner_len
    lead = real_part.shape[:-1]
    real_part = real_part.reshape(lead + (outer_len, inner_len))
    imag_part = imag_part.reshape(lead + (outer_len, inner_len))
    table_real, table_imag = dft_table(inner_len, 1.0)
    real_part, imag_part = complex_apply(
        "bu,...tu->...tb", table_real, table_imag, real_part, imag_part
    )
    freq_idx = jnp.asarray(spectral_order(outer_len), dtype=jnp.int32)[:, None]
    inner_idx = jnp.arange(inner_len, dtype=jnp.int32)[None, :]
    cos_part, sin_part = twiddle(freq_idx * inner_idx, length)
    real_part, imag_part = rotate(real_part, imag_part, cos_part, sin_part)
    real_part, imag_part = whole_inverse(
        jnp.swapaxes(real_part, -1, -2), jnp.swapaxes(imag_part, -1, -2), outer_len
    )
    real_part = jnp.swapaxes(real_part, -1, -2)
    imag_part = jnp.swapaxes(imag_part, -1, -2)
    return (real_part.reshape(lead + (length,)), imag_part.reshape(lead + (length,)))


def owner_conv(stacked, groups, samples):
    chan_rows = stacked.shape[1]
    own_rows = chan_rows // groups
    span = groups * samples
    pieces = stacked.reshape(2, groups, own_rows, samples)
    rows_whole = lax.all_to_all(pieces, "seq", split_axis=1, concat_axis=3, tiled=True).reshape(
        2, own_rows, span
    )
    padded = jnp.concatenate([rows_whole, jnp.zeros_like(rows_whole)], axis=2)
    spec_real, spec_imag = whole_forward(padded, jnp.zeros_like(padded), 2 * span)
    prod_real = spec_real[0] * spec_real[1] - spec_imag[0] * spec_imag[1]
    prod_imag = spec_real[0] * spec_imag[1] + spec_imag[0] * spec_real[1]
    back_real, back_imag = whole_inverse(prod_real, prod_imag, 2 * span)
    conv_rows = back_real[:, :span]
    return lax.all_to_all(conv_rows, "seq", split_axis=1, concat_axis=0, tiled=True)


def per_device(signal, gating, response, skip_gain, mixing_weight):
    chan_rows, samples = signal.shape
    groups = lax.axis_size("seq")
    full_len = 2 * groups * samples
    stacked = jnp.stack([signal, response])
    conv = owner_conv(stacked, groups, samples)
    conv = conv / full_len
    mixed_in = gating * (conv + skip_gain[:, None] * signal)
    return lax.psum_scatter(
        jnp.dot(
            mixing_weight,
            mixed_in,
            precision=lax.Precision.HIGHEST,
            preferred_element_type=jnp.float32,
        ),
        "chan",
        scatter_dimension=0,
        tiled=True,
    )


def solution(mesh):
    in_specs = (P("chan", "seq"), P("chan", "seq"), P("chan", "seq"), P("chan"), P(None, "chan"))
    out_specs = P("chan", "seq")
    return jax.shard_map(
        per_device, mesh=mesh, in_specs=in_specs, out_specs=out_specs, check_vma=False
    )
```

profile of v0, /device:TPU:0, one launch (start us, length us, event | category | flops | bytes accessed | tf_op | source)
XLA Modules:
  0.0 486.4 jit_solution(6807660299492079792)
XLA Ops:
  6.5 0.0 copy-start
  6.5 4.6 pad_maximum_fusion
  11.1 0.0 copy-start.7
  11.1 7.4 %all-to-all-start = ((f32[2,8,8,8192]{3,2,0,1:T(8,128)}), f32[2,8,8,8192]{3,2,0,1:T(8,128)}, u32[]{:S(2)}, u32[]{:S(2)}) async-start(f32[2,8,8,8192]{3,2,0,1:T(8,128)} %pad_maximum_fusion), calls=%async_computation | async-start | bytes 8388608 | tf_op jit(solution)/shard_map/all_to_all | solution.py:96
  18.6 0.0 reduce-scatter.4.cloned.1.call-start
  18.6 0.1 sine_negate_fusion.1
  18.7 0.1 fusion.149
  18.7 0.0 copy-done.7
  18.7 2.1 fusion.70
  20.8 3.4 fusion.69
  24.3 8.9 %fusion.34 = f32[2,8,128,128,8]{3,4,2,1,0:T(8,128)} fusion(), kind=kOutput, calls=%fused_computation.58 | convolution fusion | flops 201327552 | bytes 8388608 | tf_op jit(solution)/shard_map/kn,...n->...k/dot_general | solution.py:31
  33.2 78.7 %all-to-all-done = f32[2,8,8,8192]{3,2,0,1:T(8,128)} async-done(((f32[2,8,8,8192]{3,2,0,1:T(8,128)}), f32[2,8,8,8192]{3,2,0,1:T(8,128)}, u32[]{:S(2)}, u32[]{:S(2)}) %all-to-all-start) | async-done | bytes 4194336 | tf_op jit(solution)/shard_map/all_to_all | solution.py:96
  111.8 6.6 %copy.47 = f32[2,1,8,8,8192]{4,3,2,0,1:T(8,128)} copy(f32[2,1,8,8,8192]{4,2,0,3,1:T(8,128)} %bitcast.3) | data formatting | bytes 8388608 | tf_op jit(solution)/shard_map/all_to_all | solution.py:96
  118.4 4.0 reshape.255
  122.4 2.7 pad_bitcast_fusion
  125.1 4.9 %copy.100 = f32[2,8,1024,128]{3,2,1,0:T(8,128)} copy(f32[2,8,1024,128]{3,1,2,0:T(8,128)S(1)} %pad_bitcast_fusion) | data formatting | bytes 16777216
  130.0 8.7 %copy.74 = f32[2,8,128,8,128]{4,3,2,1,0:T(8,128)} copy(f32[2,8,128,8,128]{2,4,3,1,0:T(8,128)} %bitcast.216) | data formatting | bytes 16777216 | tf_op jit(solution)/shard_map/reshape | solution.py:50
  138.6 12.5 %fusion.4 = f32[2,8,128,128,8]{3,4,2,1,0:T(8,128)} fusion(f32[2,8,128,8,128]{4,3,2,1,0:T(8,128)} %copy.74), kind=kOutput, calls=%fused_computation.14 | convolution fusion | flops 201327552 | bytes 16777216 | tf_op jit(solution)/shard_map/kn,...n->...k/dot_general | solution.py:32
  151.1 0.0 copy-done.1
  151.1 9.3 %fusion.6 = f32[2,8,128,128,8]{3,4,2,1,0:T(8,128)} fusion(f32[2,8,128,8,128]{4,3,2,1,0:T(8,128)S(1)} %copy-done.1), kind=kOutput, calls=%fused_computation.16 | convolution fusion | flops 201327488 | bytes 16777216 | tf_op jit(solution)/shard_map/kn,...n->...k/dot_general | solution.py:31
  160.4 15.3 %fusion.2 = (f32[2,8,128,8,128]{4,3,2,1,0:T(8,128)}, f32[2,8,128,8,128]{4,3,2,1,0:T(8,128)S(1)}) fusion(f32[8,128]{1,0:T(8,128)S(1)} %get-tuple-element.19, f32[8,128]{1,0:T(8,128)S(1)} %get-tuple-element.20, f32[2,8,128,128,8]{3,4,2,1,0:T(8,128)} %fusion.4, f32[2,8,128,128,8]{3,4,2,1,0:T(8,128)} %fusion.6, f32[2,8,128,128,8]{3,4,2,1,0:T(8,128)} %fusion.34), kind=kOutput, calls=%fused_computation.10 | convolution fusion | flops 218104704 | bytes 41951232 | tf_op jit(solution)/shard_map/kn,...n->...k/dot_general | solution.py:32
  175.7 11.1 %fusion.8 = f32[2,8,128,8,128]{2,4,3,1,0:T(8,128)} fusion(f32[2,8,128,8,128]{4,3,2,1,0:T(8,128)S(1)} %get-tuple-element.6), kind=kOutput, calls=%fused_computation.19 | convolution fusion | flops 3221454848 | bytes 16777216 | tf_op jit(solution)/shard_map/ub,...tb->...tu/dot_general | solution.py:32
  186.8 0.0 slice-start.1
  186.8 8.8 %fusion.10 = f32[2,8,128,8,128]{2,4,3,1,0:T(8,128)S(1)} fusion(f32[2,8,128,8,128]{4,3,2,1,0:T(8,128)S(1)} %get-tuple-element.6), kind=kOutput, calls=%fused_computation.21 | convolution fusion | flops 3221471232 | bytes 16777216 | tf_op jit(solution)/shard_map/ub,...tb->...tu/dot_general | solution.py:31
  195.7 0.0 slice-done
  195.7 0.0 slice-done.1
  195.7 13.0 %fusion.39 = f32[2,8,128,8,128]{2,4,3,1,0:T(8,128)} fusion(f32[2,8,128,8,128]{2,4,3,1,0:T(8,128)} %fusion.8, f32[2,8,128,8,128]{4,3,2,1,0:T(8,128)S(1)} %bitcast.211), kind=kOutput, calls=%fused_computation.61 | convolution fusion | flops 3223568384 | bytes 25165824 | tf_op jit(solution)/shard_map/ub,...tb->...tu/dot_general | solution.py:32
  208.7 10.7 %fusion.36 = f32[2,8,128,8,128]{2,4,3,1,0:T(8,128)} fusion(f32[2,8,128,8,128]{2,4,3,1,0:T(8,128)S(1)} %fusion.10, f32[2,8,128,8,128]{4,3,2,1,0:T(8,128)S(1)} %bitcast.211), kind=kOutput, calls=%fused_computation.60 | convolution fusion | flops 3223552000 | bytes 25165824 | tf_op jit(solution)/shard_map/ub,...tb->...tu/dot_general | solution.py:31
  219.4 7.0 %fusion = (f32[2,8,1024,128]{3,2,1,0:T(8,128)S(1)}, f32[2,8,1024,128]{3,2,1,0:T(8,128)S(1)}) fusion(f32[2,8,128,8,128]{2,4,3,1,0:T(8,128)} %fusion.36, f32[2,8,128,8,128]{2,4,3,1,0:T(8,128)} %fusion.39, f32[1024,128]{1,0:T(8,128)S(1)} %get-tuple-element.18, f32[1024,128]{1,0:T(8,128)S(1)} %get-tuple-element.17), kind=kLoop, calls=%fused_computation.4 | loop fusion | flops 12582912 | bytes 34603008 | tf_op jit(solution)/shard_map/sub | solution.py:17
  226.5 9.7 %fusion.88 = f32[2,8,1024,128]{3,2,1,0:T(8,128)} fusion(f32[2,8,1024,128]{3,2,1,0:T(8,128)S(1)} %get-tuple-element.7), kind=kOutput, calls=%fused_computation.116 | convolution fusion | flops 3221454848 | bytes 16777216 | tf_op jit(solution)/shard_map/ub,...tb->...tu/dot_general | solution.py:31
  236.2 7.8 %fusion.86 = f32[2,8,1024,128]{3,2,1,0:T(8,128)S(1)} fusion(f32[2,8,1024,128]{3,2,1,0:T(8,128)S(1)} %get-tuple-element.8), kind=kOutput, calls=%fused_computation.114 | convolution fusion | flops 3221454848 | bytes 16777216 | tf_op jit(solution)/shard_map/ub,...tb->...tu/dot_general | solution.py:32
  244.0 11.4 %convolution_subtract_fusion = f32[2,8,1024,128]{3,2,1,0:T(8,128)} fusion(f32[2,8,1024,128]{3,2,1,0:T(8,128)} %fusion.88, f32[2,8,1024,128]{3,2,1,0:T(8,128)S(1)} %get-tuple-element.8), kind=kOutput, calls=%fused_computation.63 | convolution fusion | flops 3223568384 | bytes 25165824 | tf_op jit(solution)/shard_map/ub,...tb->...tu/dot_general | solution.py:31
  255.4 9.5 %convolution_add_fusion = f32[2,8,1024,128]{3,2,1,0:T(8,128)} fusion(f32[2,8,1024,128]{3,2,1,0:T(8,128)S(1)} %fusion.86, f32[2,8,1024,128]{3,2,1,0:T(8,128)S(1)} %get-tuple-element.7), kind=kOutput, calls=%fused_computation.62 | convolution fusion | flops 3223568384 | bytes 25165824 | tf_op jit(solution)/shard_map/ub,...tb->...tu/dot_general | solution.py:32
  264.9 0.0 copy-done.2
  264.9 4.2 multiply_subtract_fusion
  269.1 3.8 fusion.22
  272.9 3.8 fusion.20
  276.8 0.0 copy-start.4
  276.8 0.0 copy-start.5
  276.8 3.8 fusion.44
  280.6 0.0 copy-done.4
  280.6 0.0 copy-done.5
  280.6 5.2 %fusion.18 = (f32[8,128,1024]{1,2,0:T(8,128)S(1)}, f32[8,128,1024]{1,2,0:T(8,128)S(1)}) fusion(f32[8,1024,128]{2,1,0:T(8,128)S(1)} %fusion.44, f32[128,1024]{0,1:T(8,128)S(1)} %copy-done.5, f32[128,1024]{0,1:T(8,128)S(1)} %copy-done.4, f32[8,1024,128]{2,1,0:T(8,128)S(1)} %fusion.20, f32[1,8,1024,128]{3,2,1,0:T(8,128)S(1)} %get-tuple-element.9), kind=kOutput, calls=%fused_computation.37 | convolution fusion | flops 1618182144 | bytes 22020096 | tf_op jit(solution)/shard_map/bu,...tu->...tb/dot_general | solution.py:32
  285.9 7.0 %fusion.84 = f32[8,128,8,128]{3,1,2,0:T(8,128)S(1)} fusion(f32[8,128,8,128]{1,3,2,0:T(8,128)S(1)} %bitcast.212), kind=kOutput, calls=%fused_computation.112 | convolution fusion | flops 1610842112 | bytes 8388608 | tf_op jit(solution)/shard_map/bu,...tu->...tb/dot_general | solution.py:31
  292.9 7.3 %fusion.82 = f32[8,128,8,128]{3,1,2,0:T(8,128)S(1)} fusion(f32[8,128,8,128]{1,3,2,0:T(8,128)S(1)} %bitcast.214), kind=kOutput, calls=%fused_computation.110 | convolution fusion | flops 1610842112 | bytes 8388608 | tf_op jit(solution)/shard_map/bu,...tu->...tb/dot_general | solution.py:32
  300.2 7.1 %convolution_subtract_fusion.1 = f32[8,128,8,128]{3,1,2,0:T(8,128)S(1)} fusion(f32[8,128,8,128]{3,1,2,0:T(8,128)S(1)} %fusion.84, f32[8,128,8,128]{1,3,2,0:T(8,128)S(1)} %bitcast.215), kind=kOutput, calls=%fused_computation.67 | convolution fusion | flops 1611890688 | bytes 12582912 | tf_op jit(solution)/shard_map/bu,...tu->...tb/dot_general | solution.py:31
  307.3 7.3 %fusion.16 = (f32[8,128,128,8]{2,1,3,0:T(8,128)S(1)}, f32[8,128,128,8]{2,1,3,0:T(8,128)S(1)}) fusion(f32[8,128,8,128]{3,1,2,0:T(8,128)S(1)} %convolution_subtract_fusion.1, f32[128,8]{0,1:T(8,128)S(1)} %get-tuple-element.21, f32[128,8]{0,1:T(8,128)S(1)} %get-tuple-element.22, f32[8,128,8,128]{3,1,2,0:T(8,128)S(1)} %fusion.82, ...), kind=kOutput, calls=%fused_computation.31 | convolution fusion | flops 1618182144 | bytes 20979712 | tf_op jit(solution)/shard_map/bu,...tu->...tb/dot_general | solution.py:32
  314.6 6.6 %fusion.28 = f32[8,128,128,8]{2,3,1,0:T(8,128)S(1)} fusion(f32[8,128,128,8]{2,1,3,0:T(8,128)S(1)} %get-tuple-element.14), kind=kOutput, calls=%fused_computation.49 | convolution fusion | flops 100664192 | bytes 8388608 | tf_op jit(solution)/shard_map/kn,...n->...k/dot_general | solution.py:31
  321.2 6.9 %subtract_bitcast_fusion = f32[8,128,8,128]{3,2,1,0:T(8,128)} fusion(f32[8,128,128,8]{2,3,1,0:T(8,128)S(1)} %fusion.28, f32[8,128,128,8]{2,1,3,0:T(8,128)S(1)} %get-tuple-element.13), kind=kOutput, calls=%fused_computation.53 | convolution fusion | flops 101712768 | bytes 12582912 | tf_op jit(solution)/shard_map/kn,...n->...k/dot_general | solution.py:31
  328.1 5.4 %copy.75 = f32[8,128,8,128]{1,3,2,0:T(8,128)} copy(f32[8,128,8,128]{3,2,1,0:T(8,128)} %subtract_bitcast_fusion) | data formatting | bytes 8388608 | tf_op jit(solution)/shard_map/reshape | solution.py:88
  333.5 4.6 copy.101
  338.1 0.0 copy-start.3
  338.1 0.0 copy-start.6
  338.1 0.0 copy-start.8
  338.1 0.1 slice.32
  338.3 52.3 %all_to_all.28 = f32[8,8,8192]{2,0,1:T(8,128)S(1)} all-to-all(f32[8,8,8192]{2,0,1:T(8,128)S(1)} %bitcast.219), channel_id=1, replica_groups=mesh['seq'=8,'chan'=4] {'seq'}, dimensions={1} | all-to-all | bytes 4194304 | tf_op jit(solution)/shard_map/all_to_all | solution.py:105
  390.6 0.0 copy-done
  390.6 0.0 copy-done.3
  390.6 0.0 copy-done.6
  390.6 0.0 copy-done.8
  390.6 9.1 %convolution_bitcast_fusion = f32[256,8192]{0,1:T(8,128)} fusion(f32[256,64]{0,1:T(8,128)S(1)} %copy-done, f32[64,8192]{1,0:T(8,128)S(1)} %copy-done.6, f32[64,8192]{1,0:T(8,128)S(1)} %copy-done.3, f32[8,8,8192]{2,0,1:T(8,128)S(1)} %all_to_all.28, f32[64]{0:T(128)S(1)} %copy-done.8), kind=kOutput, calls=%fused_computation | convolution fusion | flops 1612709888 | bytes 14745856 | tf_op jit(solution)/shard_map/dot_general | solution.py:117
  399.7 8.9 %copy.76 = f32[256,8192]{1,0:T(8,128)} copy(f32[256,8192]{0,1:T(8,128)} %convolution_bitcast_fusion) | data formatting | bytes 16777216
  408.6 0.0 reduce-scatter.4.cloned.1.call-update
  408.6 70.6 %reduce-scatter.4.cloned.1.call-done = f32[64,8192]{1,0:T(8,128)} async-done(((f32[256,8192]{1,0:T(8,128)}), f32[64,8192]{1,0:T(8,128)}) %reduce-scatter.4.cloned.1.call-update) | async-done | bytes 2097168 | tf_op jit(solution)/shard_map/reduce_scatter | solution.py:116
  (4 shorter events, 0.0 us)
Async XLA Ops:
  6.5 384.1 %copy-start = (f32[256,64]{0,1:T(8,128)S(1)}, f32[256,64]{0,1:T(8,128)}, u32[]{:S(2)}) copy-start(f32[256,64]{0,1:T(8,128)} %param.13) | copy-start | bytes 196612
  11.1 7.6 %copy-start.7 = (s32[1024]{0:T(1024)S(1)}, s32[1024]{0:T(1024)}, u32[]{:S(2)}) copy-start(s32[1024]{0:T(1024)} %constant.100.clone) | copy-start | bytes 12292
  11.1 100.7 %all-to-all-start = ((f32[2,8,8,8192]{3,2,0,1:T(8,128)}), f32[2,8,8,8192]{3,2,0,1:T(8,128)}, u32[]{:S(2)}, u32[]{:S(2)}) async-start(f32[2,8,8,8192]{3,2,0,1:T(8,128)} %pad_maximum_fusion), calls=%async_computation | async-start | bytes 8388608 | tf_op jit(solution)/shard_map/all_to_all | solution.py:96
  18.6 460.7 %reduce-scatter.4.cloned.1.call-start = ((), (), s32[]{:S(2)}) async-start(), calls=%async_computation.3 | async-start | bytes 10485760 | tf_op jit(solution)/shard_map/reduce_scatter | solution.py:116
  138.6 12.5 %copy-start.1 = (f32[2,8,128,8,128]{4,3,2,1,0:T(8,128)S(1)}, f32[2,8,128,8,128]{4,3,2,1,0:T(8,128)}, u32[]{:S(2)}) copy-start(f32[2,8,128,8,128]{4,3,2,1,0:T(8,128)} %copy.74) | copy-start | bytes 25165828
  175.7 20.0 %slice-start = ((s8[8388608]{0:T(1024)(128)(4,1)}), s8[4194304]{0:T(1024)(128)(4,1)S(1)}, s32[]{:S(2)}) async-start(s8[8388608]{0:T(1024)(128)(4,1)} %bitcast.210), calls=%async_computation.4 | async-start | bytes 8388608
  186.8 8.9 %slice-start.1 = ((s8[8388608]{0:T(1024)(128)(4,1)}), s8[4194304]{0:T(1024)(128)(4,1)S(1)}, s32[]{:S(2)}) async-start(s8[8388608]{0:T(1024)(128)(4,1)} %bitcast.210), calls=%async_computation.5 | async-start | bytes 8388608
  255.4 9.5 %copy-start.2 = (f32[2,8,1024,128]{3,2,1,0:T(8,128)S(1)}, f32[2,8,1024,128]{3,2,1,0:T(8,128)}, u32[]{:S(2)}) copy-start(f32[2,8,1024,128]{3,2,1,0:T(8,128)} %convolution_subtract_fusion) | copy-start | bytes 25165828
  276.8 3.9 copy-start.4
  276.8 3.9 copy-start.5
  338.1 52.5 %copy-start.3 = (f32[64,8192]{1,0:T(8,128)S(1)}, f32[64,8192]{1,0:T(8,128)}, u32[]{:S(2)}) copy-start(f32[64,8192]{1,0:T(8,128)} %param.9) | copy-start | bytes 6291460
  338.1 52.5 %copy-start.6 = (f32[64,8192]{1,0:T(8,128)S(1)}, f32[64,8192]{1,0:T(8,128)}, u32[]{:S(2)}) copy-start(f32[64,8192]{1,0:T(8,128)} %param.10) | copy-start | bytes 6291460
  338.1 52.5 %copy-start.8 = (f32[64]{0:T(128)S(1)}, f32[64]{0:T(128)}, u32[]{:S(2)}) copy-start(f32[64]{0:T(128)} %param.12) | copy-start | bytes 772
Sparse Core Ops, SparseCore 0:
  408.8 70.4 reduce-scatter.3
where the time goes:
time: 490 us; the launch traced here: 486 us
  matrix products  196 us (40%)
  waiting for transfers between devices  149 us (30%)
  blocking collectives  52.3 us (11%)
  local copies, waits for them, and re-layouts  45.9 us (9%)
  other arithmetic  21.5 us (4%)
  between operations  13.9 us (3%)
  starting transfers between devices  7.45 us (2%)
    all_to_all x1, waiting for transfers between devices, owner_conv(): lax.all_to_all(pieces, 'seq', split_axis=1, concat_axis=3, tiled=True)  78.7 us
    reduce_scatter x1, waiting for transfers between devices, per_device(): lax.psum_scatter(jnp.dot(mixing_weight, mixed_in, precision=lax.Precision...  70.6 us
    all_to_all x1, blocking collectives, owner_conv(): lax.all_to_all(conv_rows, 'seq', split_axis=1, concat_axis=0, tiled=True)  52.3 us
    dot_general x5, matrix products, complex_apply(): contract(table_imag, real_part)  47.6 us
    dot_general x6, matrix products, complex_apply(): contract(table_real, real_part) - contract(table_imag, imag_part)  47.5 us
    dot_general x6, matrix products, complex_apply(): contract(table_imag, imag_part)  46.6 us
    dot_general x5, matrix products, complex_apply(): contract(table_real, imag_part) + contract(table_imag, real_part)  45.3 us
    unnamed x26, local copies, waits for them, and re-layouts  21.2 us
  transfers between devices with their start and end apart: 2, of which 2 were waited for; matrix products, arithmetic and copies ran while one was open for 3% of the time, Pallas kernels for 0%

commit v1 on v0

--- a/solution.py
+++ b/solution.py
@@ -5,6 +5,21 @@
 import numpy as np
 from jax import lax
 from jax.sharding import PartitionSpec as P
+from jax.lax import axis_index, axis_size, ppermute
+
+
+def skins_start(obj, array_axis, row_data):
+    y_new, front = (obj.shape[:array_axis], obj.shape[array_axis + 1 :])
+    value_now = obj.reshape(*y_new, row_data, -1, *front)
+    arr_now = jnp.moveaxis(value_now, array_axis, 0)
+    return arr_now
+
+
+def lay_files_here(state, k_dim):
+    spare = list(state.shape[1:])
+    spare[k_dim] *= state.shape[0]
+    formed = jnp.moveaxis(state, 0, k_dim).reshape(spare)
+    return formed
 
 
 def twiddle(number, period):
@@ -93,9 +108,25 @@
     own_rows = chan_rows // groups
     span = groups * samples
     pieces = stacked.reshape(2, groups, own_rows, samples)
-    rows_whole = lax.all_to_all(pieces, "seq", split_axis=1, concat_axis=3, tiled=True).reshape(
-        2, own_rows, span
-    )
+
+    def deliver_edge(block_here, shard_axis, sheet, unit):
+        piece_out = axis_size(shard_axis)
+        o_now = axis_index(shard_axis)
+        low, r1 = (piece_out, o_now)
+        passed = skins_start(block_here, sheet, low)
+        seen = [passed[r1]]
+        dd = 1
+        while dd < low:
+            w1 = passed[(r1 + dd) % low]
+            kept_arr = ppermute(w1, shard_axis, perm=[(p, (p + dd) % low) for p in range(low)])
+            seen.append(kept_arr)
+            dd = dd + 1
+        taken_in = jnp.stack(seen, axis=0)
+        passed = taken_in[(r1 - jnp.arange(low)) % low]
+        main = lay_files_here(passed, unit)
+        return main
+
+    rows_whole = deliver_edge(pieces, "seq", 1, 3).reshape(2, own_rows, span)
     padded = jnp.concatenate([rows_whole, jnp.zeros_like(rows_whole)], axis=2)
     spec_real, spec_imag = whole_forward(padded, jnp.zeros_like(padded), 2 * span)
     prod_real = spec_real[0] * spec_real[1] - spec_imag[0] * spec_imag[1]

time: 490 us -> 500 us (1.020); the launches traced: 486 us -> 491 us
  waiting for transfers between devices: 149 us -> 101 us
  blocking collectives: 52.3 us -> 80.3 us
  local copies, waits for them, and re-layouts: 45.9 us -> 62.3 us
  starting transfers between devices: 7.45 us -> 13.7 us
    all_to_all x1 -> x0, waiting for transfers between devices: 78.7 us -> none  [owner_conv(): lax.all_to_all(pieces, 'seq', split_axis=1, concat_axis=3, tiled=True)]
    ppermute x0 -> x7, waiting for transfers between devices: none -> 30.6 us  [deliver_edge(): ppermute(w1, shard_axis, perm=[(p, (p + dd) % low) for p in range(low)])]
    all_to_all x1, blocking collectives: 52.3 us -> 80.3 us  [owner_conv(): lax.all_to_all(conv_rows, 'seq', split_axis=1, concat_axis=0, tiled=True)]
    ppermute x0 -> x7, starting transfers between devices: none -> 13.7 us  [deliver_edge(): ppermute(w1, shard_axis, perm=[(p, (p + dd) % low) for p in range(low)])]
    unnamed x26 -> x36, local copies, waits for them, and re-layouts: 21.2 us -> 31.5 us
    all_to_all x1 -> x0, starting transfers between devices: 7.41 us -> none  [owner_conv(): lax.all_to_all(pieces, 'seq', split_axis=1, concat_axis=3, tiled=True)]
    transpose x0 -> x1, local copies, waits for them, and re-layouts: none -> 6.62 us  [lay_files_here(): formed = jnp.moveaxis(state, 0, k_dim).reshape(spare)]
    all_to_all x1 -> x0, local copies, waits for them, and re-layouts: 6.56 us -> none  [owner_conv(): lax.all_to_all(pieces, 'seq', split_axis=1, concat_axis=3, tiled=True)]
  transfers between devices with their start and end apart: 2 -> 8, of which waited for: 2 -> 3; matrix products, arithmetic and copies ran while one was open for 3% -> 6% of each run, Pallas kernels for 0% -> 0%
where the time goes in v1:
time: 500 us; the launch traced here: 491 us
  matrix products  196 us (39%)
  waiting for transfers between devices  101 us (20%)
  blocking collectives  80.3 us (16%)
  local copies, waits for them, and re-layouts  62.3 us (12%)
  other arithmetic  23.3 us (5%)
  between operations  14.1 us (3%)
  starting transfers between devices  13.7 us (3%)
    all_to_all x1, blocking collectives, owner_conv(): lax.all_to_all(conv_rows, 'seq', split_axis=1, concat_axis=0, tiled=True)  80.3 us
    reduce_scatter x1, waiting for transfers between devices, per_device(): lax.psum_scatter(jnp.dot(mixing_weight, mixed_in, precision=lax.Precision...  70.5 us
    dot_general x6, matrix products, complex_apply(): contract(table_real, real_part) - contract(table_imag, imag_part)  47.6 us
    dot_general x5, matrix products, complex_apply(): contract(table_imag, real_part)  47.4 us
    dot_general x6, matrix products, complex_apply(): contract(table_imag, imag_part)  46.7 us
    dot_general x5, matrix products, complex_apply(): contract(table_real, imag_part) + contract(table_imag, real_part)  45.2 us
    unnamed x36, local copies, waits for them, and re-layouts  31.5 us
    ppermute x7, waiting for transfers between devices, deliver_edge(): ppermute(w1, shard_axis, perm=[(p, (p + dd) % low) for p in range(low)])  30.6 us
  transfers between devices with their start and end apart: 8, of which 3 were waited for; matrix products, arithmetic and copies ran while one was open for 6% of the time, Pallas kernels for 0%

profile of v1, /device:TPU:0, one launch (start us, length us, event | category | flops | bytes accessed | tf_op | source)
XLA Modules:
  0.0 490.7 jit_solution(15497374753521021417)
XLA Ops:
  6.5 3.7 fusion.63
  10.2 3.0 collective-permute-start
  13.2 1.6 collective-permute-start.1
  14.8 2.6 collective-permute-start.2
  17.3 1.2 collective-permute-start.3
  18.6 2.6 collective-permute-start.4
  21.2 0.1 sine_negate_fusion.1
  21.3 0.1 fusion.182
  21.3 0.0 copy-start.9
  21.3 1.9 fusion.66
  23.2 1.0 fusion.78
  24.2 2.1 fusion.87
  26.3 3.3 fusion.86
  29.6 8.9 %fusion.34 = f32[2,8,128,128,8]{3,4,2,1,0:T(8,128)} fusion(), kind=kOutput, calls=%fused_computation.74 | convolution fusion | flops 201327552 | bytes 8388608 | tf_op jit(solution)/shard_map/kn,...n->...k/dot_general | solution.py:46
  38.5 1.3 collective-permute-start.5
  39.9 1.9 bitcast_dynamic-update-slice_fusion.6
  41.8 1.4 collective-permute-start.6
  43.2 1.9 bitcast_dynamic-update-slice_fusion.5
  45.1 28.5 %collective-permute-done.2 = f32[2,1,8,8192]{3,2,0,1:T(8,128)} collective-permute-done((f32[2,1,8,8192]{3,2,0,1:T(8,128)}, f32[2,1,8,8192]{3,2,0,1:T(8,128)}, u32[]{:S(2)}, u32[]{:S(2)}) %collective-permute-start.2) | collective-permute-done | bytes 524320 | tf_op jit(solution)/shard_map/ppermute | solution.py:121
  73.6 1.9 bitcast_dynamic-update-slice_fusion.4
  75.5 1.9 bitcast_dynamic-update-slice_fusion.3
  77.4 1.9 bitcast_dynamic-update-slice_fusion.2
  79.2 0.8 bitcast_dynamic-update-slice_fusion.1
  80.1 2.0 collective-permute-done.6
  82.1 0.9 bitcast_dynamic-update-slice_fusion
  83.0 4.9 %gather_fusion = f32[8,2,8,8192]{3,2,1,0:T(8,128)} fusion(f32[8,2,8,8192]{3,2,1,0:T(8,128)} %bitcast.19, s32[1024]{0:T(1024)S(1)} %pad_clamp_fusion), kind=kCustom, calls=%fused_computation | custom fusion | bytes 8388640 | tf_op jit(solution)/shard_map/gather | solution.py:125
  87.9 6.6 %copy.52 = f32[2,1,8,8,8192]{4,3,2,0,1:T(8,128)} copy(f32[2,1,8,8,8192]{4,2,0,3,1:T(8,128)} %bitcast.262) | data formatting | bytes 8388608 | tf_op jit(solution)/shard_map/transpose | solution.py:21
  94.6 4.1 reshape_reshape.4
  98.7 2.7 pad_bitcast_fusion
  101.4 4.9 copy.105
  106.3 8.7 %copy.79 = f32[2,8,128,8,128]{4,3,2,1,0:T(8,128)} copy(f32[2,8,128,8,128]{2,4,3,1,0:T(8,128)} %bitcast.258) | data formatting | bytes 16777216 | tf_op jit(solution)/shard_map/reshape | solution.py:65
  115.0 12.3 %fusion.4 = f32[2,8,128,128,8]{3,4,2,1,0:T(8,128)} fusion(f32[2,8,128,8,128]{4,3,2,1,0:T(8,128)} %copy.79), kind=kOutput, calls=%fused_computation.31 | convolution fusion | flops 201327552 | bytes 16777216 | tf_op jit(solution)/shard_map/kn,...n->...k/dot_general | solution.py:47
  127.2 9.3 %fusion.6 = f32[2,8,128,128,8]{3,4,2,1,0:T(8,128)} fusion(f32[2,8,128,8,128]{4,3,2,1,0:T(8,128)S(1)} %copy-done.1), kind=kOutput, calls=%fused_computation.33 | convolution fusion | flops 201327488 | bytes 16777216 | tf_op jit(solution)/shard_map/kn,...n->...k/dot_general | solution.py:46
  136.5 15.5 %fusion.2 = (f32[2,8,128,8,128]{4,3,2,1,0:T(8,128)}, f32[2,8,128,8,128]{4,3,2,1,0:T(8,128)S(1)}) fusion(f32[8,128]{1,0:T(8,128)S(1)} %get-tuple-element.25, f32[8,128]{1,0:T(8,128)S(1)} %get-tuple-element.26, f32[2,8,128,128,8]{3,4,2,1,0:T(8,128)} %fusion.4, f32[2,8,128,128,8]{3,4,2,1,0:T(8,128)} %fusion.6, f32[2,8,128,128,8]{3,4,2,1,0:T(8,128)} %fusion.34), kind=kOutput, calls=%fused_computation.27 | convolution fusion | flops 218104704 | bytes 41951232 | tf_op jit(solution)/shard_map/kn,...n->...k/dot_general | solution.py:47
  152.0 10.8 %fusion.8 = f32[2,8,128,8,128]{2,4,3,1,0:T(8,128)} fusion(f32[2,8,128,8,128]{4,3,2,1,0:T(8,128)S(1)} %get-tuple-element.6), kind=kOutput, calls=%fused_computation.36 | convolution fusion | flops 3221454848 | bytes 16777216 | tf_op jit(solution)/shard_map/ub,...tb->...tu/dot_general | solution.py:47
  162.8 8.8 %fusion.10 = f32[2,8,128,8,128]{2,4,3,1,0:T(8,128)S(1)} fusion(f32[2,8,128,8,128]{4,3,2,1,0:T(8,128)S(1)} %get-tuple-element.6), kind=kOutput, calls=%fused_computation.38 | convolution fusion | flops 3221471232 | bytes 16777216 | tf_op jit(solution)/shard_map/ub,...tb->...tu/dot_general | solution.py:46
  171.7 13.1 %fusion.39 = f32[2,8,128,8,128]{2,4,3,1,0:T(8,128)} fusion(f32[2,8,128,8,128]{2,4,3,1,0:T(8,128)} %fusion.8, f32[2,8,128,8,128]{4,3,2,1,0:T(8,128)S(1)} %bitcast.250), kind=kOutput, calls=%fused_computation.77 | convolution fusion | flops 3223568384 | bytes 25165824 | tf_op jit(solution)/shard_map/ub,...tb->...tu/dot_general | solution.py:47
  184.8 10.7 %fusion.36 = f32[2,8,128,8,128]{2,4,3,1,0:T(8,128)} fusion(f32[2,8,128,8,128]{2,4,3,1,0:T(8,128)S(1)} %fusion.10, f32[2,8,128,8,128]{4,3,2,1,0:T(8,128)S(1)} %bitcast.250), kind=kOutput, calls=%fused_computation.76 | convolution fusion | flops 3223552000 | bytes 25165824 | tf_op jit(solution)/shard_map/ub,...tb->...tu/dot_general | solution.py:46
  195.5 7.0 %fusion = (f32[2,8,1024,128]{3,2,1,0:T(8,128)S(1)}, f32[2,8,1024,128]{3,2,1,0:T(8,128)S(1)}) fusion(f32[2,8,128,8,128]{2,4,3,1,0:T(8,128)} %fusion.36, f32[2,8,128,8,128]{2,4,3,1,0:T(8,128)} %fusion.39, f32[1024,128]{1,0:T(8,128)S(1)} %get-tuple-element.24, f32[1024,128]{1,0:T(8,128)S(1)} %get-tuple-element.23), kind=kLoop, calls=%fused_computation.21 | loop fusion | flops 12582912 | bytes 34603008 | tf_op jit(solution)/shard_map/sub | solution.py:32
  202.6 9.8 %fusion.105 = f32[2,8,1024,128]{3,2,1,0:T(8,128)} fusion(f32[2,8,1024,128]{3,2,1,0:T(8,128)S(1)} %get-tuple-element.7), kind=kOutput, calls=%fused_computation.156 | convolution fusion | flops 3221454848 | bytes 16777216 | tf_op jit(solution)/shard_map/ub,...tb->...tu/dot_general | solution.py:46
  212.4 7.8 %fusion.103 = f32[2,8,1024,128]{3,2,1,0:T(8,128)S(1)} fusion(f32[2,8,1024,128]{3,2,1,0:T(8,128)S(1)} %get-tuple-element.8), kind=kOutput, calls=%fused_computation.154 | convolution fusion | flops 3221454848 | bytes 16777216 | tf_op jit(solution)/shard_map/ub,...tb->...tu/dot_general | solution.py:47
  220.1 11.5 %convolution_subtract_fusion = f32[2,8,1024,128]{3,2,1,0:T(8,128)} fusion(f32[2,8,1024,128]{3,2,1,0:T(8,128)} %fusion.105, f32[2,8,1024,128]{3,2,1,0:T(8,128)S(1)} %get-tuple-element.8), kind=kOutput, calls=%fused_computation.79 | convolution fusion | flops 3223568384 | bytes 25165824 | tf_op jit(solution)/shard_map/ub,...tb->...tu/dot_general | solution.py:46
  231.6 9.6 %convolution_add_fusion = f32[2,8,1024,128]{3,2,1,0:T(8,128)} fusion(f32[2,8,1024,128]{3,2,1,0:T(8,128)S(1)} %fusion.103, f32[2,8,1024,128]{3,2,1,0:T(8,128)S(1)} %get-tuple-element.7), kind=kOutput, calls=%fused_computation.78 | convolution fusion | flops 3223568384 | bytes 25165824 | tf_op jit(solution)/shard_map/ub,...tb->...tu/dot_general | solution.py:47
  241.2 4.2 multiply_subtract_fusion
  245.3 3.8 fusion.22
  249.2 3.8 fusion.20
  253.0 3.8 fusion.44
  256.9 5.2 %fusion.18 = (f32[8,128,1024]{1,2,0:T(8,128)S(1)}, f32[8,128,1024]{1,2,0:T(8,128)S(1)}) fusion(f32[8,1024,128]{2,1,0:T(8,128)S(1)} %fusion.44, f32[128,1024]{0,1:T(8,128)S(1)} %copy-done.6, f32[128,1024]{0,1:T(8,128)S(1)} %copy-done.5, f32[8,1024,128]{2,1,0:T(8,128)S(1)} %fusion.20, f32[1,8,1024,128]{3,2,1,0:T(8,128)S(1)} %get-tuple-element.9), kind=kOutput, calls=%fused_computation.53 | convolution fusion | flops 1618182144 | bytes 22020096 | tf_op jit(solution)/shard_map/bu,...tu->...tb/dot_general | solution.py:47
  262.1 7.0 %fusion.101 = f32[8,128,8,128]{3,1,2,0:T(8,128)S(1)} fusion(f32[8,128,8,128]{1,3,2,0:T(8,128)S(1)} %bitcast.251), kind=kOutput, calls=%fused_computation.152 | convolution fusion | flops 1610842112 | bytes 8388608 | tf_op jit(solution)/shard_map/bu,...tu->...tb/dot_general | solution.py:46
  269.2 7.3 %fusion.99 = f32[8,128,8,128]{3,1,2,0:T(8,128)S(1)} fusion(f32[8,128,8,128]{1,3,2,0:T(8,128)S(1)} %bitcast.253), kind=kOutput, calls=%fused_computation.150 | convolution fusion | flops 1610842112 | bytes 8388608 | tf_op jit(solution)/shard_map/bu,...tu->...tb/dot_general | solution.py:47
  276.4 7.1 %convolution_subtract_fusion.1 = f32[8,128,8,128]{3,1,2,0:T(8,128)S(1)} fusion(f32[8,128,8,128]{3,1,2,0:T(8,128)S(1)} %fusion.101, f32[8,128,8,128]{1,3,2,0:T(8,128)S(1)} %bitcast.254), kind=kOutput, calls=%fused_computation.83 | convolution fusion | flops 1611890688 | bytes 12582912 | tf_op jit(solution)/shard_map/bu,...tu->...tb/dot_general | solution.py:46
  283.5 7.3 %fusion.16 = (f32[8,128,128,8]{2,1,3,0:T(8,128)S(1)}, f32[8,128,128,8]{2,1,3,0:T(8,128)S(1)}) fusion(f32[8,128,8,128]{3,1,2,0:T(8,128)S(1)} %convolution_subtract_fusion.1, f32[128,8]{0,1:T(8,128)S(1)} %get-tuple-element.27, f32[128,8]{0,1:T(8,128)S(1)} %get-tuple-element.28, f32[8,128,8,128]{3,1,2,0:T(8,128)S(1)} %fusion.99, ...), kind=kOutput, calls=%fused_computation.47 | convolution fusion | flops 1618182144 | bytes 20979712 | tf_op jit(solution)/shard_map/bu,...tu->...tb/dot_general | solution.py:47
  290.8 6.6 %fusion.28 = f32[8,128,128,8]{2,3,1,0:T(8,128)S(1)} fusion(f32[8,128,128,8]{2,1,3,0:T(8,128)S(1)} %get-tuple-element.14), kind=kOutput, calls=%fused_computation.65 | convolution fusion | flops 100664192 | bytes 8388608 | tf_op jit(solution)/shard_map/kn,...n->...k/dot_general | solution.py:46
  297.4 6.9 %subtract_bitcast_fusion = f32[8,128,8,128]{3,2,1,0:T(8,128)} fusion(f32[8,128,128,8]{2,3,1,0:T(8,128)S(1)} %fusion.28, f32[8,128,128,8]{2,1,3,0:T(8,128)S(1)} %get-tuple-element.13), kind=kOutput, calls=%fused_computation.69 | convolution fusion | flops 101712768 | bytes 12582912 | tf_op jit(solution)/shard_map/kn,...n->...k/dot_general | solution.py:46
  304.3 5.4 %copy.80 = f32[8,128,8,128]{1,3,2,0:T(8,128)} copy(f32[8,128,8,128]{3,2,1,0:T(8,128)} %subtract_bitcast_fusion) | data formatting | bytes 8388608 | tf_op jit(solution)/shard_map/reshape | solution.py:103
  309.7 4.6 copy.106
  314.4 0.0 copy-start.4
  314.4 0.0 copy-start.10
  314.4 0.1 slice.34
  314.5 80.3 %all_to_all.13 = f32[8,8,8192]{2,0,1:T(8,128)S(1)} all-to-all(f32[8,8,8192]{2,0,1:T(8,128)S(1)} %bitcast.265), channel_id=1, replica_groups=mesh['seq'=8,'chan'=4] {'seq'}, dimensions={1} | all-to-all | bytes 4194304 | tf_op jit(solution)/shard_map/all_to_all | solution.py:136
  394.8 9.1 %convolution_bitcast_fusion = f32[256,8192]{0,1:T(8,128)} fusion(f32[256,64]{0,1:T(8,128)S(1)} %copy-done, f32[64,8192]{1,0:T(8,128)S(1)} %copy-done.7, f32[64,8192]{1,0:T(8,128)S(1)} %copy-done.4, f32[8,8,8192]{2,0,1:T(8,128)S(1)} %all_to_all.13, f32[64]{0:T(128)S(1)} %copy-done.10), kind=kOutput, calls=%fused_computation.1 | convolution fusion | flops 1612709888 | bytes 14745856 | tf_op jit(solution)/shard_map/dot_general | solution.py:148
  403.9 9.0 %copy.81 = f32[256,8192]{1,0:T(8,128)} copy(f32[256,8192]{0,1:T(8,128)} %convolution_bitcast_fusion) | data formatting | bytes 16777216
  412.9 0.0 reduce-scatter.4.cloned.1.call-update
  412.9 70.5 %reduce-scatter.4.cloned.1.call-done = f32[64,8192]{1,0:T(8,128)} async-done(((f32[256,8192]{1,0:T(8,128)}), f32[64,8192]{1,0:T(8,128)}) %reduce-scatter.4.cloned.1.call-update) | async-done | bytes 2097168 | tf_op jit(solution)/shard_map/reduce_scatter | solution.py:147
  (32 shorter events, 0.1 us)
Async XLA Ops:
  6.5 388.3 %copy-start = (f32[256,64]{0,1:T(8,128)S(1)}, f32[256,64]{0,1:T(8,128)}, u32[]{:S(2)}) copy-start(f32[256,64]{0,1:T(8,128)} %param.13) | copy-start | bytes 196612
  6.5 14.8 %copy-start.3 = (f32[64,8192]{1,0:T(8,128)S(1)}, f32[64,8192]{1,0:T(8,128)}, u32[]{:S(2)}) copy-start(f32[64,8192]{1,0:T(8,128)} %param.9) | copy-start | bytes 6291460
  6.5 476.9 %reduce-scatter.4.cloned.1.call-start = ((), (), s32[]{:S(2)}) async-start(), calls=%async_computation.2 | async-start | bytes 10485760 | tf_op jit(solution)/shard_map/reduce_scatter | solution.py:147
  10.2 28.3 %collective-permute-start = (f32[2,1,8,8192]{3,2,0,1:T(8,128)}, f32[2,1,8,8192]{3,2,0,1:T(8,128)}, u32[]{:S(2)}, u32[]{:S(2)}) collective-permute-start(f32[2,1,8,8192]{3,2,0,1:T(8,128)} %get-tuple-element.16), channel_id=1, source_target_pairs={{0,4},{4,8},{8,12},{12,16},{16,20},{20,24},{24,28},{28,0},{1,5},{5... | collective-permute-start | bytes 1572872 | tf_op jit(solution)/shard_map/ppermute | solution.py:121
  13.2 28.6 %collective-permute-start.1 = (f32[2,1,8,8192]{3,2,0,1:T(8,128)}, f32[2,1,8,8192]{3,2,0,1:T(8,128)}, u32[]{:S(2)}, u32[]{:S(2)}) collective-permute-start(f32[2,1,8,8192]{3,2,0,1:T(8,128)} %get-tuple-element.17), channel_id=1, source_target_pairs={{0,8},{4,12},{8,16},{12,20},{16,24},{20,28},{24,0},{28,4},{1,9},{5... | collective-permute-start | bytes 1572872 | tf_op jit(solution)/shard_map/ppermute | solution.py:121
  14.8 58.8 %collective-permute-start.2 = (f32[2,1,8,8192]{3,2,0,1:T(8,128)}, f32[2,1,8,8192]{3,2,0,1:T(8,128)}, u32[]{:S(2)}, u32[]{:S(2)}) collective-permute-start(f32[2,1,8,8192]{3,2,0,1:T(8,128)} %get-tuple-element.18), channel_id=1, source_target_pairs={{0,12},{4,16},{8,20},{12,24},{16,28},{20,0},{24,4},{28,8},{1,13},{... | collective-permute-start | bytes 1572872 | tf_op jit(solution)/shard_map/ppermute | solution.py:121
  17.3 58.1 %collective-permute-start.3 = (f32[2,1,8,8192]{3,2,0,1:T(8,128)}, f32[2,1,8,8192]{3,2,0,1:T(8,128)}, u32[]{:S(2)}, u32[]{:S(2)}) collective-permute-start(f32[2,1,8,8192]{3,2,0,1:T(8,128)} %get-tuple-element.19), channel_id=1, source_target_pairs={{0,16},{4,20},{8,24},{12,28},{16,0},{20,4},{24,8},{28,12},{1,17},{... | collective-permute-start | bytes 1572872 | tf_op jit(solution)/shard_map/ppermute | solution.py:121
  18.6 58.8 %collective-permute-start.4 = (f32[2,1,8,8192]{3,2,0,1:T(8,128)}, f32[2,1,8,8192]{3,2,0,1:T(8,128)}, u32[]{:S(2)}, u32[]{:S(2)}) collective-permute-start(f32[2,1,8,8192]{3,2,0,1:T(8,128)} %get-tuple-element.20), channel_id=1, source_target_pairs={{0,20},{4,24},{8,28},{12,0},{16,4},{20,8},{24,12},{28,16},{1,21},{... | collective-permute-start | bytes 1572872 | tf_op jit(solution)/shard_map/ppermute | solution.py:121
  21.3 2.9 copy-start.9
  29.6 12.2 %copy-start.8 = (f32[2,1,8,8192]{3,2,0,1:T(8,128)S(1)}, f32[2,1,8,8192]{3,2,0,1:T(8,128)}, u32[]{:S(2)}) copy-start(f32[2,1,8,8192]{3,2,0,1:T(8,128)} %get-tuple-element.15) | copy-start | bytes 1572868
  38.5 40.7 %collective-permute-start.5 = (f32[2,1,8,8192]{3,2,0,1:T(8,128)S(1)}, f32[2,1,8,8192]{3,2,0,1:T(8,128)S(1)}, u32[]{:S(2)}, u32[]{:S(2)}) collective-permute-start(f32[2,1,8,8192]{3,2,0,1:T(8,128)S(1)} %fusion.78), channel_id=1, source_target_pairs={{0,24},{4,28},{8,0},{12,4},{16,8},{20,12},{24,16},{28,20},{1,25},{... | collective-permute-start | bytes 1572872 | tf_op jit(solution)/shard_map/ppermute | solution.py:121
  41.8 40.4 %collective-permute-start.6 = (f32[2,1,8,8192]{3,2,0,1:T(8,128)S(1)}, f32[2,1,8,8192]{3,2,0,1:T(8,128)S(1)}, u32[]{:S(2)}, u32[]{:S(2)}) collective-permute-start(f32[2,1,8,8192]{3,2,0,1:T(8,128)S(1)} %copy-done.8), channel_id=1, source_target_pairs={{0,28},{4,0},{8,4},{12,8},{16,12},{20,16},{24,20},{28,24},{1,29},{... | collective-permute-start | bytes 1572872 | tf_op jit(solution)/shard_map/ppermute | solution.py:121
  115.0 12.3 %copy-start.1 = (f32[2,8,128,8,128]{4,3,2,1,0:T(8,128)S(1)}, f32[2,8,128,8,128]{4,3,2,1,0:T(8,128)}, u32[]{:S(2)}) copy-start(f32[2,8,128,8,128]{4,3,2,1,0:T(8,128)} %copy.79) | copy-start | bytes 25165828
  152.0 19.7 %slice-start = ((s8[8388608]{0:T(1024)(128)(4,1)}), s8[4194304]{0:T(1024)(128)(4,1)S(1)}, s32[]{:S(2)}) async-start(s8[8388608]{0:T(1024)(128)(4,1)} %bitcast.249), calls=%async_computation.3 | async-start | bytes 8388608
  162.8 8.9 %slice-start.1 = ((s8[8388608]{0:T(1024)(128)(4,1)}), s8[4194304]{0:T(1024)(128)(4,1)S(1)}, s32[]{:S(2)}) async-start(s8[8388608]{0:T(1024)(128)(4,1)} %bitcast.249), calls=%async_computation.4 | async-start | bytes 8388608
  231.6 9.6 %copy-start.2 = (f32[2,8,1024,128]{3,2,1,0:T(8,128)S(1)}, f32[2,8,1024,128]{3,2,1,0:T(8,128)}, u32[]{:S(2)}) copy-start(f32[2,8,1024,128]{3,2,1,0:T(8,128)} %convolution_subtract_fusion) | copy-start | bytes 25165828
  253.0 3.9 copy-start.5
  253.0 3.9 copy-start.6
  314.4 80.4 %copy-start.4 = (f32[64,8192]{1,0:T(8,128)S(1)}, f32[64,8192]{1,0:T(8,128)}, u32[]{:S(2)}) copy-start(f32[64,8192]{1,0:T(8,128)} %param.9) | copy-start | bytes 6291460
  314.4 80.4 %copy-start.7 = (f32[64,8192]{1,0:T(8,128)S(1)}, f32[64,8192]{1,0:T(8,128)}, u32[]{:S(2)}) copy-start(f32[64,8192]{1,0:T(8,128)} %param.10) | copy-start | bytes 6291460
  314.4 80.4 %copy-start.10 = (f32[64]{0:T(128)S(1)}, f32[64]{0:T(128)}, u32[]{:S(2)}) copy-start(f32[64]{0:T(128)} %param.12) | copy-start | bytes 772
Sparse Core Ops, SparseCore 0:
  413.1 70.3 reduce-scatter.3
